TPU v7x, 32 devices: a whole 2x2x4 slice. The times are simulated.
32 devices in a mesh: vol: 2 (over core), wide: 8 (over z, x), narrow: 2 (over y).
Axes of the slice: x: 2, y: 2, z: 4, core: 2. Of those that a mesh axis runs over, the one named last changes fastest.
Arguments:
- forcing: float32 [2, 4, 384, 1024], P(None, 'vol', 'narrow', 'wide'), may hold values from -180 to 180
- material_ids: int32 [4, 384, 1024], P('vol', 'narrow', 'wide'), may hold values from 0 to 7
- materials: float32 [8], replicated, may hold values from 0.5 to 2
- boundary_operator: bfloat16 [1024, 32768], P('wide', 'narrow'), may hold values from -0.03125 to 0.03125
Outputs:
- pressure: float32 [2, 4, 384, 1024], P(None, 'vol', 'narrow', 'wide')
- traction: float32 [1024, 2], P(('wide', 'narrow'), 'vol')
All inputs are finite; a program needn't handle non-finite values.
Results may differ from a plain program's by a relative error of at most 0.0031.
Values may be sent and summed in bfloat16 or wider, within the bound.
No kernel may reach another device: no remote copies, remote signals or barrier semaphores. Data moves between devices by JAX's collectives and lax.ppermute only.
A program may use at most 128 MiB of HBM per device.

v0:
```python
import jax
import jax.numpy as jnp
from jax import lax
from jax.sharding import PartitionSpec as P

BY = 16
RY = 1
RX = 64
MAT = 8
ITERS = 2
lower_edge = 0.25
upper_edge = 1.75
mass_ratio = 26.0
couple_gain = 40.0


def with_halo(shard, sides, width):
    for axis, dim in sides:
        peers, length = (lax.axis_size(axis), shard.shape[dim])
        up = [(i, (i + 1) % peers) for i in range(peers - 1)]
        down = [(j, i) for i, j in up]
        last = lax.slice_in_dim(shard, length - width, length, axis=dim)
        first = lax.slice_in_dim(shard, 0, width, axis=dim)
        before = lax.ppermute(last, axis, up)
        after = lax.ppermute(first, axis, down)
        shard = jnp.concatenate([before, shard, after], axis=dim)
    return shard


def from_root(shard, axis, root):
    mine = lax.axis_index(axis) == root
    return lax.psum(jnp.where(mine, shard, jnp.zeros_like(shard)), axis)


def sweep_weights():
    middle = (upper_edge + lower_edge) / 2.0
    spread = (upper_edge - lower_edge) / 2.0
    center_ratio = middle / spread
    ratio_last = 1.0 / center_ratio
    weights = [(0.0, 1.0 / middle)]
    ratio_next = 1.0 / (2.0 * center_ratio - ratio_last)
    weights.append((ratio_next * ratio_last, 2.0 * ratio_next / spread))
    return weights


def box_sum(padded):
    along = padded[..., :-2] + padded[..., 1:-1] + padded[..., 2:]
    along = along[..., :-2, :] + along[..., 1:-1, :] + along[..., 2:, :]
    return along[..., :-2, :, :] + along[..., 1:-1, :, :] + along[..., 2:, :, :]


def apply_operator(padded, center, cond_pad, conductance, diagonal):
    neighbours = box_sum(padded) - center
    weighted = box_sum(padded * cond_pad) - conductance * center
    return diagonal * center - 0.5 * (conductance * neighbours + weighted)


def relax(vol_field, source, cond_pad, conductance, diagonal):
    moved = jnp.zeros_like(vol_field)
    for keep_weight, gain_weight in sweep_weights():
        padded = with_halo(vol_field, (("vol", 1), ("wide", 3), ("narrow", 2)), 1)
        scaled = (
            source - apply_operator(padded, vol_field, cond_pad, conductance, diagonal)
        ) / diagonal
        moved = keep_weight * moved + gain_weight * scaled
        vol_field = vol_field + moved
    return vol_field


def fold_traces(mine, plane):
    return jnp.einsum(
        "ryx,kyx->rk",
        plane,
        lax.all_gather(mine, "wide", axis=2, tiled=True),
        preferred_element_type=jnp.float32,
    )


def local(forcing, material_ids, materials, boundary_operator):
    conductance = jnp.zeros(material_ids.shape, jnp.float32)
    for number in range(MAT):
        conductance = conductance + jnp.where(material_ids == number, materials[number], 0.0)
    cond_pad = with_halo(conductance, (("vol", 0), ("wide", 2), ("narrow", 1)), 1)
    diagonal = (
        0.5 * (26.0 * conductance + (box_sum(cond_pad) - conductance)) + mass_ratio * conductance
    )
    vol_count = lax.axis_size("vol")
    last_vol = vol_count - 1
    own_vol = lax.axis_index("vol")
    excite = forcing.shape[0]
    half_count = excite // vol_count
    tile_rows = boundary_operator.shape[0]
    cells_y = forcing.shape[2]
    cells_x = forcing.shape[3]
    stride = cells_y // BY
    plane = boundary_operator.reshape(tile_rows, BY, -1)
    is_top = (own_vol == last_vol).astype(jnp.float32)
    pressure = jnp.zeros(forcing.shape, jnp.float32)
    source = forcing
    traction = jnp.zeros((tile_rows // lax.axis_size("narrow"), half_count), jnp.float32)
    for outer in range(ITERS):
        pressure = relax(pressure, source, cond_pad, conductance, diagonal)
        surface = pressure[:, -1, ::stride].astype(jnp.bfloat16)
        copied = from_root(surface, "vol", last_vol)
        mine = lax.dynamic_slice_in_dim(copied, own_vol * half_count, half_count, 0)
        partial_rows = fold_traces(mine, plane)
        summed = lax.psum(partial_rows, "narrow")
        share = summed.shape[0] // lax.axis_size("narrow")
        traction = lax.dynamic_slice_in_dim(summed, lax.axis_index("narrow") * share, share, 0)
        if outer + 1 < ITERS:
            shared = lax.all_gather(traction, "vol", axis=1, tiled=True)
            placed = jnp.transpose(shared).reshape(excite, RY, RX)
            placed = jnp.pad(placed, ((0, 0), (0, cells_y - RY), (0, cells_x - RX)))
            source = forcing.at[:, -1].add(couple_gain * is_top * placed)
    return (pressure, traction)


def solution(mesh):
    placed = (
        P(None, "vol", "narrow", "wide"),
        P("vol", "narrow", "wide"),
        P(),
        P("wide", "narrow"),
    )
    return jax.shard_map(
        local,
        mesh=mesh,
        in_specs=placed,
        out_specs=(P(None, "vol", "narrow", "wide"), P(("wide", "narrow"), "vol")),
        check_vma=False,
    )
```

profile of v0, /device:TPU:0, one launch (start us, length us, event | category | flops | bytes accessed | tf_op | source)
XLA Modules:
  0.0 236.0 jit_solution(11555738974021824176)
XLA Ops:
  2.3 6.8 %broadcast_multiply_fusion.5 = (f32[2,192,128]{2,1,0:T(8,128)}, f32[2,192,128]{2,1,0:T(8,128)S(1)}) fusion(f32[]{:T(128)} %bitcast.7, s32[2,192,128]{2,1,0:T(8,128)} %param.7, f32[]{:T(128)} %bitcast.6, f32[]{:T(128)} %bitcast.5, f32[]{:T(128)} %bitcast.4, f32[]{:T(128)} %bitcast.3, f32[]{:T(128)} %bitcast.2, f32[]{:T(128)} %bitcast.1, f32[]{:T(128)} %bitcast), kind=kLoop, calls=%fused_computation.111 | loop fusion | flops 1179648 | bytes 589856 | tf_op jit(solution)/shard_map/mul | solution.py:54
  14.9 4.2 %collective-permute-start.2 = (f32[4,192,1]{2,1,0:T(8,128)S(1)}, f32[4,192,1]{2,1,0:T(8,128)S(1)}, u32[]{:S(2)}, u32[]{:S(2)}) collective-permute-start(f32[4,192,1]{2,1,0:T(8,128)S(1)} %get-tuple-element.62), channel_id=1, source_target_pairs={{0,2},{2,4},{4,6},{6,8},{8,10},{10,12},{12,14},{1,3},{3,5},{5,7},{... | collective-permute-start | bytes 9224 | tf_op jit(solution)/shard_map/ppermute | solution.py:24
  20.5 15.8 %collective-permute-done.2 = f32[4,192,1]{2,1,0:T(8,128)S(1)} collective-permute-done((f32[4,192,1]{2,1,0:T(8,128)S(1)}, f32[4,192,1]{2,1,0:T(8,128)S(1)}, u32[]{:S(2)}, u32[]{:S(2)}) %collective-permute-start.2) | collective-permute-done | bytes 3104 | tf_op jit(solution)/shard_map/ppermute | solution.py:24
  36.3 3.4 %collective-permute-start.4 = (f32[4,1,130]{2,1,0:T(1,128)S(1)}, f32[4,1,130]{2,1,0:T(1,128)S(1)}, u32[]{:S(2)}, u32[]{:S(2)}) collective-permute-start(f32[4,1,130]{2,1,0:T(1,128)S(1)} %get-tuple-element.44), channel_id=1, source_target_pairs={{0,1},{2,3},{4,5},{6,7},{8,9},{10,11},{12,13},{14,15},{16,17},{18,... | collective-permute-start | bytes 6248 | tf_op jit(solution)/shard_map/ppermute | solution.py:24
  42.4 3.0 %collective-permute-start.6 = (f32[2,1,192,128]{3,2,0,1:T(8,128)S(1)}, f32[2,1,192,128]{3,2,0,1:T(8,128)S(1)}, u32[]{:S(2)}, u32[]{:S(2)}) collective-permute-start(f32[2,1,192,128]{3,2,0,1:T(8,128)S(1)} %broadcast.51), channel_id=1, source_target_pairs={{0,16},{1,17},{2,18},{3,19},{4,20},{5,21},{6,22},{7,23},{8,24},{9,... | collective-permute-start | bytes 589832 | tf_op jit(solution)/shard_map/ppermute | solution.py:24
  50.9 5.0 %collective-permute-start.8 = (f32[2,4,192,1]{2,1,3,0:T(4,128)S(1)}, f32[2,4,192,1]{2,1,3,0:T(4,128)S(1)}, u32[]{:S(2)}, u32[]{:S(2)}) collective-permute-start(f32[2,4,192,1]{2,1,3,0:T(4,128)S(1)} %copy.19), channel_id=1, source_target_pairs={{0,2},{2,4},{4,6},{6,8},{8,10},{10,12},{12,14},{1,3},{3,5},{5,7},{... | collective-permute-start | bytes 18440 | tf_op jit(solution)/shard_map/ppermute | solution.py:24
  58.0 4.5 %collective-permute-start.10 = (f32[2,4,1,130]{3,2,0,1:T(1,128)S(1)}, f32[2,4,1,130]{3,2,0,1:T(1,128)S(1)}, u32[]{:S(2)}, u32[]{:S(2)}) collective-permute-start(f32[2,4,1,130]{3,2,0,1:T(1,128)S(1)} %get-tuple-element.42), channel_id=1, source_target_pairs={{0,1},{2,3},{4,5},{6,7},{8,9},{10,11},{12,13},{14,15},{16,17},{18,... | collective-permute-start | bytes 12488 | tf_op jit(solution)/shard_map/ppermute | solution.py:24
  65.1 3.0 %collective-permute-done.11 = f32[2,4,1,130]{3,2,0,1:T(1,128)S(1)} collective-permute-done((f32[2,4,1,130]{3,2,0,1:T(1,128)S(1)}, f32[2,4,1,130]{3,2,0,1:T(1,128)S(1)}, u32[]{:S(2)}, u32[]{:S(2)}) %collective-permute-start.11) | collective-permute-done | bytes 4192 | tf_op jit(solution)/shard_map/ppermute | solution.py:25
  78.8 4.8 %collective-permute-start.14 = (f32[2,4,192,1]{2,1,3,0:T(4,128)S(1)}, f32[2,4,192,1]{2,1,3,0:T(4,128)S(1)}, u32[]{:S(2)}, u32[]{:S(2)}) collective-permute-start(f32[2,4,192,1]{2,1,3,0:T(4,128)S(1)} %copy.24), channel_id=1, source_target_pairs={{0,2},{2,4},{4,6},{6,8},{8,10},{10,12},{12,14},{1,3},{3,5},{5,7},{... | collective-permute-start | bytes 18440 | tf_op jit(solution)/shard_map/ppermute | solution.py:24
  85.6 5.1 %collective-permute-done.15 = f32[2,4,192,1]{2,1,3,0:T(4,128)S(1)} collective-permute-done((f32[2,4,192,1]{2,1,3,0:T(4,128)S(1)}, f32[2,4,192,1]{2,1,3,0:T(4,128)S(1)}, u32[]{:S(2)}, u32[]{:S(2)}) %collective-permute-start.15) | collective-permute-done | bytes 6176 | tf_op jit(solution)/shard_map/ppermute | solution.py:25
  94.8 6.4 %copy.43 = bf16[128,16384]{0,1:T(8,128)(2,1)} copy(bf16[128,16384]{1,0:T(8,128)(2,1)} %param.9) | data formatting | bytes 8388608 | tf_op jit(solution)/shard_map/reshape | solution.py:96
  105.4 2.5 %psum.28 = bf16[2,16,128]{2,1,0:T(8,128)(2,1)S(1)} all-reduce(bf16[2,16,128]{2,1,0:T(8,128)(2,1)S(1)} %select_bitcast_fusion.1), channel_id=1, replica_groups=mesh['vol'=2,'wide'=8,'narrow'=2] {'vol'}, use_global_device_ids=true, to_apply=%region_0.1 | all-reduce | flops 4096 | bytes 16384 | tf_op jit(solution)/shard_map/psum | solution.py:32
  107.9 26.0 %all_gather.9 = bf16[1,16,1024]{2,1,0:T(8,128)(2,1)S(1)} all-gather(bf16[1,16,128]{2,1,0:T(8,128)(2,1)S(1)} %constant_dynamic-slice_fusion.3), channel_id=1, replica_groups=mesh['vol'=2,'wide'=8,'narrow'=2] {'wide'}, dimensions={2}, use_global_device_ids=true | all-gather | bytes 36864 | tf_op jit(solution)/shard_map/all_gather | solution.py:74
  136.6 2.9 %convolution_bitcast_fusion.1 = f32[128,1]{0,1:T(1,128)S(1)} fusion(bf16[128,16,1024]{0,2,1:T(8,128)(2,1)} %bitcast.31, bf16[16,1024,1]{1,0,2:T(8,128)(2,1)S(1)} %bitcast.33), kind=kOutput, calls=%fused_computation.5 | convolution fusion | flops 4194304 | bytes 4227584 | tf_op jit(solution)/shard_map/ryx,kyx->rk/dot_general | solution.py:71
  139.4 5.5 %psum.29 = f32[128,1]{0,1:T(1,128)S(1)} all-reduce(f32[128,1]{0,1:T(1,128)S(1)} %convolution_bitcast_fusion.1), channel_id=1, replica_groups=mesh['vol'=2,'wide'=8,'narrow'=2] {'narrow'}, use_global_device_ids=true, to_apply=%region_1.2 | all-reduce | flops 128 | bytes 1024 | tf_op jit(solution)/shard_map/psum | solution.py:107
  147.7 4.5 %collective-permute-start.20 = (f32[2,4,192,1]{2,1,3,0:T(4,128)S(1)}, f32[2,4,192,1]{2,1,3,0:T(4,128)S(1)}, u32[]{:S(2)}, u32[]{:S(2)}) collective-permute-start(f32[2,4,192,1]{2,1,3,0:T(4,128)S(1)} %copy.31), channel_id=1, source_target_pairs={{0,2},{2,4},{4,6},{6,8},{8,10},{10,12},{12,14},{1,3},{3,5},{5,7},{... | collective-permute-start | bytes 18440 | tf_op jit(solution)/shard_map/ppermute | solution.py:24
  155.7 3.9 %collective-permute-start.22 = (f32[2,4,1,130]{3,2,0,1:T(1,128)S(1)}, f32[2,4,1,130]{3,2,0,1:T(1,128)S(1)}, u32[]{:S(2)}, u32[]{:S(2)}) collective-permute-start(f32[2,4,1,130]{3,2,0,1:T(1,128)S(1)} %get-tuple-element.38), channel_id=1, source_target_pairs={{0,1},{2,3},{4,5},{6,7},{8,9},{10,11},{12,13},{14,15},{16,17},{18,... | collective-permute-start | bytes 12488 | tf_op jit(solution)/shard_map/ppermute | solution.py:24
  161.1 4.2 %collective-permute-done.23 = f32[2,4,1,130]{3,2,0,1:T(1,128)S(1)} collective-permute-done((f32[2,4,1,130]{3,2,0,1:T(1,128)S(1)}, f32[2,4,1,130]{3,2,0,1:T(1,128)S(1)}, u32[]{:S(2)}, u32[]{:S(2)}) %collective-permute-start.23) | collective-permute-done | bytes 4192 | tf_op jit(solution)/shard_map/ppermute | solution.py:25
  175.3 4.8 %collective-permute-start.26 = (f32[2,4,192,1]{2,1,3,0:T(4,128)S(1)}, f32[2,4,192,1]{2,1,3,0:T(4,128)S(1)}, u32[]{:S(2)}, u32[]{:S(2)}) collective-permute-start(f32[2,4,192,1]{2,1,3,0:T(4,128)S(1)} %copy.35), channel_id=1, source_target_pairs={{0,2},{2,4},{4,6},{6,8},{8,10},{10,12},{12,14},{1,3},{3,5},{5,7},{... | collective-permute-start | bytes 18440 | tf_op jit(solution)/shard_map/ppermute | solution.py:24
  182.0 4.6 %collective-permute-done.27 = f32[2,4,192,1]{2,1,3,0:T(4,128)S(1)} collective-permute-done((f32[2,4,192,1]{2,1,3,0:T(4,128)S(1)}, f32[2,4,192,1]{2,1,3,0:T(4,128)S(1)}, u32[]{:S(2)}, u32[]{:S(2)}) %collective-permute-start.27) | collective-permute-done | bytes 6176 | tf_op jit(solution)/shard_map/ppermute | solution.py:25
  190.8 4.2 %collective-permute-done.29 = f32[2,4,1,130]{3,2,0,1:T(1,128)S(1)} collective-permute-done((f32[2,4,1,130]{3,2,0,1:T(1,128)S(1)}, f32[2,4,1,130]{3,2,0,1:T(1,128)S(1)}, u32[]{:S(2)}, u32[]{:S(2)}) %collective-permute-start.29) | collective-permute-done | bytes 4192 | tf_op jit(solution)/shard_map/ppermute | solution.py:25
  200.8 26.0 %all_gather.11 = bf16[1,16,1024]{2,1,0:T(8,128)(2,1)S(1)} all-gather(bf16[1,16,128]{2,1,0:T(8,128)(2,1)S(1)} %constant_dynamic-slice_fusion.1), channel_id=1, replica_groups=mesh['vol'=2,'wide'=8,'narrow'=2] {'wide'}, dimensions={2}, use_global_device_ids=true | all-gather | bytes 36864 | tf_op jit(solution)/shard_map/all_gather | solution.py:74
  226.8 2.9 %convolution_bitcast_fusion = f32[128,1]{0,1:T(1,128)S(1)} fusion(bf16[128,16,1024]{0,2,1:T(8,128)(2,1)} %bitcast.32, bf16[16,1024,1]{1,0,2:T(8,128)(2,1)S(1)} %bitcast.34), kind=kOutput, calls=%fused_computation.4 | convolution fusion | flops 4194304 | bytes 4227584 | tf_op jit(solution)/shard_map/ryx,kyx->rk/dot_general | solution.py:71
  229.7 4.9 %psum.31 = f32[128,1]{0,1:T(1,128)S(1)} all-reduce(f32[128,1]{0,1:T(1,128)S(1)} %convolution_bitcast_fusion), channel_id=1, replica_groups=mesh['vol'=2,'wide'=8,'narrow'=2] {'narrow'}, use_global_device_ids=true, to_apply=%region_3.4 | all-reduce | flops 128 | bytes 1024 | tf_op jit(solution)/shard_map/psum | solution.py:107
  (158 shorter events, 75.4 us)
Async XLA Ops:
  9.1 3.7 %collective-permute-start = (f32[1,192,128]{2,1,0:T(8,128)S(1)}, f32[1,192,128]{2,1,0:T(8,128)S(1)}, u32[]{:S(2)}, u32[]{:S(2)}) collective-permute-start(f32[1,192,128]{2,1,0:T(8,128)S(1)} %get-tuple-element.64), channel_id=1, source_target_pairs={{0,16},{1,17},{2,18},{3,19},{4,20},{5,21},{6,22},{7,23},{8,24},{9,... | collective-permute-start | bytes 294920 | tf_op jit(solution)/shard_map/ppermute | solution.py:24
  14.9 21.3 %collective-permute-start.2 = (f32[4,192,1]{2,1,0:T(8,128)S(1)}, f32[4,192,1]{2,1,0:T(8,128)S(1)}, u32[]{:S(2)}, u32[]{:S(2)}) collective-permute-start(f32[4,192,1]{2,1,0:T(8,128)S(1)} %get-tuple-element.62), channel_id=1, source_target_pairs={{0,2},{2,4},{4,6},{6,8},{8,10},{10,12},{12,14},{1,3},{3,5},{5,7},{... | collective-permute-start | bytes 9224 | tf_op jit(solution)/shard_map/ppermute | solution.py:24
  19.2 17.1 %collective-permute-start.3 = (f32[4,192,1]{2,1,0:T(8,128)S(1)}, f32[4,192,1]{2,1,0:T(8,128)S(1)}, u32[]{:S(2)}, u32[]{:S(2)}) collective-permute-start(f32[4,192,1]{2,1,0:T(8,128)S(1)} %get-tuple-element.63), channel_id=1, source_target_pairs={{2,0},{4,2},{6,4},{8,6},{10,8},{12,10},{14,12},{3,1},{5,3},{7,5},{... | collective-permute-start | bytes 9224 | tf_op jit(solution)/shard_map/ppermute | solution.py:25
  36.3 9.1 %collective-permute-start.4 = (f32[4,1,130]{2,1,0:T(1,128)S(1)}, f32[4,1,130]{2,1,0:T(1,128)S(1)}, u32[]{:S(2)}, u32[]{:S(2)}) collective-permute-start(f32[4,1,130]{2,1,0:T(1,128)S(1)} %get-tuple-element.44), channel_id=1, source_target_pairs={{0,1},{2,3},{4,5},{6,7},{8,9},{10,11},{12,13},{14,15},{16,17},{18,... | collective-permute-start | bytes 6248 | tf_op jit(solution)/shard_map/ppermute | solution.py:24
  39.8 5.7 %collective-permute-start.5 = (f32[4,1,130]{2,1,0:T(1,128)S(1)}, f32[4,1,130]{2,1,0:T(1,128)S(1)}, u32[]{:S(2)}, u32[]{:S(2)}) collective-permute-start(f32[4,1,130]{2,1,0:T(1,128)S(1)} %get-tuple-element.45), channel_id=1, source_target_pairs={{1,0},{3,2},{5,4},{7,6},{9,8},{11,10},{13,12},{15,14},{17,16},{19,... | collective-permute-start | bytes 6248 | tf_op jit(solution)/shard_map/ppermute | solution.py:25
  41.1 5.1 %collective-permute-start.7 = (f32[2,1,192,128]{3,2,0,1:T(8,128)S(1)}, f32[2,1,192,128]{3,2,0,1:T(8,128)S(1)}, u32[]{:S(2)}, u32[]{:S(2)}) collective-permute-start(f32[2,1,192,128]{3,2,0,1:T(8,128)S(1)} %broadcast.51), channel_id=1, source_target_pairs={{16,0},{17,1},{18,2},{19,3},{20,4},{21,5},{22,6},{23,7},{24,8},{25... | collective-permute-start | bytes 589832 | tf_op jit(solution)/shard_map/ppermute | solution.py:25
  42.4 4.1 %collective-permute-start.6 = (f32[2,1,192,128]{3,2,0,1:T(8,128)S(1)}, f32[2,1,192,128]{3,2,0,1:T(8,128)S(1)}, u32[]{:S(2)}, u32[]{:S(2)}) collective-permute-start(f32[2,1,192,128]{3,2,0,1:T(8,128)S(1)} %broadcast.51), channel_id=1, source_target_pairs={{0,16},{1,17},{2,18},{3,19},{4,20},{5,21},{6,22},{7,23},{8,24},{9,... | collective-permute-start | bytes 589832 | tf_op jit(solution)/shard_map/ppermute | solution.py:24
  49.6 8.0 %collective-permute-start.9 = (f32[2,4,192,1]{2,1,3,0:T(4,128)S(1)}, f32[2,4,192,1]{2,1,3,0:T(4,128)S(1)}, u32[]{:S(2)}, u32[]{:S(2)}) collective-permute-start(f32[2,4,192,1]{2,1,3,0:T(4,128)S(1)} %copy.20), channel_id=1, source_target_pairs={{2,0},{4,2},{6,4},{8,6},{10,8},{12,10},{14,12},{3,1},{5,3},{7,5},{... | collective-permute-start | bytes 18440 | tf_op jit(solution)/shard_map/ppermute | solution.py:25
  50.9 6.4 %collective-permute-start.8 = (f32[2,4,192,1]{2,1,3,0:T(4,128)S(1)}, f32[2,4,192,1]{2,1,3,0:T(4,128)S(1)}, u32[]{:S(2)}, u32[]{:S(2)}) collective-permute-start(f32[2,4,192,1]{2,1,3,0:T(4,128)S(1)} %copy.19), channel_id=1, source_target_pairs={{0,2},{2,4},{4,6},{6,8},{8,10},{10,12},{12,14},{1,3},{3,5},{5,7},{... | collective-permute-start | bytes 18440 | tf_op jit(solution)/shard_map/ppermute | solution.py:24
  58.0 7.0 %collective-permute-start.10 = (f32[2,4,1,130]{3,2,0,1:T(1,128)S(1)}, f32[2,4,1,130]{3,2,0,1:T(1,128)S(1)}, u32[]{:S(2)}, u32[]{:S(2)}) collective-permute-start(f32[2,4,1,130]{3,2,0,1:T(1,128)S(1)} %get-tuple-element.42), channel_id=1, source_target_pairs={{0,1},{2,3},{4,5},{6,7},{8,9},{10,11},{12,13},{14,15},{16,17},{18,... | collective-permute-start | bytes 12488 | tf_op jit(solution)/shard_map/ppermute | solution.py:24
  62.6 5.5 %collective-permute-start.11 = (f32[2,4,1,130]{3,2,0,1:T(1,128)S(1)}, f32[2,4,1,130]{3,2,0,1:T(1,128)S(1)}, u32[]{:S(2)}, u32[]{:S(2)}) collective-permute-start(f32[2,4,1,130]{3,2,0,1:T(1,128)S(1)} %get-tuple-element.43), channel_id=1, source_target_pairs={{1,0},{3,2},{5,4},{7,6},{9,8},{11,10},{13,12},{15,14},{17,16},{19,... | collective-permute-start | bytes 12488 | tf_op jit(solution)/shard_map/ppermute | solution.py:25
  78.8 6.5 %collective-permute-start.14 = (f32[2,4,192,1]{2,1,3,0:T(4,128)S(1)}, f32[2,4,192,1]{2,1,3,0:T(4,128)S(1)}, u32[]{:S(2)}, u32[]{:S(2)}) collective-permute-start(f32[2,4,192,1]{2,1,3,0:T(4,128)S(1)} %copy.24), channel_id=1, source_target_pairs={{0,2},{2,4},{4,6},{6,8},{8,10},{10,12},{12,14},{1,3},{3,5},{5,7},{... | collective-permute-start | bytes 18440 | tf_op jit(solution)/shard_map/ppermute | solution.py:24
  84.0 6.7 %collective-permute-start.15 = (f32[2,4,192,1]{2,1,3,0:T(4,128)S(1)}, f32[2,4,192,1]{2,1,3,0:T(4,128)S(1)}, u32[]{:S(2)}, u32[]{:S(2)}) collective-permute-start(f32[2,4,192,1]{2,1,3,0:T(4,128)S(1)} %copy.25), channel_id=1, source_target_pairs={{2,0},{4,2},{6,4},{8,6},{10,8},{12,10},{14,12},{3,1},{5,3},{7,5},{... | collective-permute-start | bytes 18440 | tf_op jit(solution)/shard_map/ppermute | solution.py:25
  91.9 9.4 %collective-permute-start.16 = (f32[2,4,1,130]{3,2,0,1:T(1,128)S(1)}, f32[2,4,1,130]{3,2,0,1:T(1,128)S(1)}, u32[]{:S(2)}, u32[]{:S(2)}) collective-permute-start(f32[2,4,1,130]{3,2,0,1:T(1,128)S(1)} %get-tuple-element.40), channel_id=1, source_target_pairs={{0,1},{2,3},{4,5},{6,7},{8,9},{10,11},{12,13},{14,15},{16,17},{18,... | collective-permute-start | bytes 12488 | tf_op jit(solution)/shard_map/ppermute | solution.py:24
  93.5 7.7 %collective-permute-start.17 = (f32[2,4,1,130]{3,2,0,1:T(1,128)S(1)}, f32[2,4,1,130]{3,2,0,1:T(1,128)S(1)}, u32[]{:S(2)}, u32[]{:S(2)}) collective-permute-start(f32[2,4,1,130]{3,2,0,1:T(1,128)S(1)} %get-tuple-element.41), channel_id=1, source_target_pairs={{1,0},{3,2},{5,4},{7,6},{9,8},{11,10},{13,12},{15,14},{17,16},{19,... | collective-permute-start | bytes 12488 | tf_op jit(solution)/shard_map/ppermute | solution.py:25
  134.0 11.0 %collective-permute-start.18 = (f32[2,1,192,128]{3,2,0,1:T(8,128)S(1)}, f32[2,1,192,128]{3,2,0,1:T(8,128)S(1)}, u32[]{:S(2)}, u32[]{:S(2)}) collective-permute-start(f32[2,1,192,128]{3,2,0,1:T(8,128)S(1)} %get-tuple-element.56), channel_id=1, source_target_pairs={{0,16},{1,17},{2,18},{3,19},{4,20},{5,21},{6,22},{7,23},{8,24},{9,... | collective-permute-start | bytes 589832 | tf_op jit(solution)/shard_map/ppermute | solution.py:24
  135.3 9.7 %collective-permute-start.19 = (f32[2,1,192,128]{3,2,0,1:T(8,128)S(1)}, f32[2,1,192,128]{3,2,0,1:T(8,128)S(1)}, u32[]{:S(2)}, u32[]{:S(2)}) collective-permute-start(f32[2,1,192,128]{3,2,0,1:T(8,128)S(1)} %get-tuple-element.57), channel_id=1, source_target_pairs={{16,0},{17,1},{18,2},{19,3},{20,4},{21,5},{22,6},{23,7},{24,8},{25... | collective-permute-start | bytes 589832 | tf_op jit(solution)/shard_map/ppermute | solution.py:25
  146.4 8.1 %collective-permute-start.21 = (f32[2,4,192,1]{2,1,3,0:T(4,128)S(1)}, f32[2,4,192,1]{2,1,3,0:T(4,128)S(1)}, u32[]{:S(2)}, u32[]{:S(2)}) collective-permute-start(f32[2,4,192,1]{2,1,3,0:T(4,128)S(1)} %copy.32), channel_id=1, source_target_pairs={{2,0},{4,2},{6,4},{8,6},{10,8},{12,10},{14,12},{3,1},{5,3},{7,5},{... | collective-permute-start | bytes 18440 | tf_op jit(solution)/shard_map/ppermute | solution.py:25
  147.7 6.4 %collective-permute-start.20 = (f32[2,4,192,1]{2,1,3,0:T(4,128)S(1)}, f32[2,4,192,1]{2,1,3,0:T(4,128)S(1)}, u32[]{:S(2)}, u32[]{:S(2)}) collective-permute-start(f32[2,4,192,1]{2,1,3,0:T(4,128)S(1)} %copy.31), channel_id=1, source_target_pairs={{0,2},{2,4},{4,6},{6,8},{8,10},{10,12},{12,14},{1,3},{3,5},{5,7},{... | collective-permute-start | bytes 18440 | tf_op jit(solution)/shard_map/ppermute | solution.py:24
  155.7 5.3 %collective-permute-start.22 = (f32[2,4,1,130]{3,2,0,1:T(1,128)S(1)}, f32[2,4,1,130]{3,2,0,1:T(1,128)S(1)}, u32[]{:S(2)}, u32[]{:S(2)}) collective-permute-start(f32[2,4,1,130]{3,2,0,1:T(1,128)S(1)} %get-tuple-element.38), channel_id=1, source_target_pairs={{0,1},{2,3},{4,5},{6,7},{8,9},{10,11},{12,13},{14,15},{16,17},{18,... | collective-permute-start | bytes 12488 | tf_op jit(solution)/shard_map/ppermute | solution.py:24
  159.7 5.5 %collective-permute-start.23 = (f32[2,4,1,130]{3,2,0,1:T(1,128)S(1)}, f32[2,4,1,130]{3,2,0,1:T(1,128)S(1)}, u32[]{:S(2)}, u32[]{:S(2)}) collective-permute-start(f32[2,4,1,130]{3,2,0,1:T(1,128)S(1)} %get-tuple-element.39), channel_id=1, source_target_pairs={{1,0},{3,2},{5,4},{7,6},{9,8},{11,10},{13,12},{15,14},{17,16},{19,... | collective-permute-start | bytes 12488 | tf_op jit(solution)/shard_map/ppermute | solution.py:25
  175.3 6.4 %collective-permute-start.26 = (f32[2,4,192,1]{2,1,3,0:T(4,128)S(1)}, f32[2,4,192,1]{2,1,3,0:T(4,128)S(1)}, u32[]{:S(2)}, u32[]{:S(2)}) collective-permute-start(f32[2,4,192,1]{2,1,3,0:T(4,128)S(1)} %copy.35), channel_id=1, source_target_pairs={{0,2},{2,4},{4,6},{6,8},{8,10},{10,12},{12,14},{1,3},{3,5},{5,7},{... | collective-permute-start | bytes 18440 | tf_op jit(solution)/shard_map/ppermute | solution.py:24
  180.4 6.2 %collective-permute-start.27 = (f32[2,4,192,1]{2,1,3,0:T(4,128)S(1)}, f32[2,4,192,1]{2,1,3,0:T(4,128)S(1)}, u32[]{:S(2)}, u32[]{:S(2)}) collective-permute-start(f32[2,4,192,1]{2,1,3,0:T(4,128)S(1)} %copy.36), channel_id=1, source_target_pairs={{2,0},{4,2},{6,4},{8,6},{10,8},{12,10},{14,12},{3,1},{5,3},{7,5},{... | collective-permute-start | bytes 18440 | tf_op jit(solution)/shard_map/ppermute | solution.py:25
  189.4 5.5 %collective-permute-start.29 = (f32[2,4,1,130]{3,2,0,1:T(1,128)S(1)}, f32[2,4,1,130]{3,2,0,1:T(1,128)S(1)}, u32[]{:S(2)}, u32[]{:S(2)}) collective-permute-start(f32[2,4,1,130]{3,2,0,1:T(1,128)S(1)} %get-tuple-element.37), channel_id=1, source_target_pairs={{1,0},{3,2},{5,4},{7,6},{9,8},{11,10},{13,12},{15,14},{17,16},{19,... | collective-permute-start | bytes 12488 | tf_op jit(solution)/shard_map/ppermute | solution.py:25
  (24 other events, 119.1 us)
where the time goes:
time: 237 us; the launch traced here: 236 us
  blocking collectives  69.3 us (29%)
  starting transfers between devices  67.3 us (28%)
  waiting for transfers between devices  43.7 us (18%)
  other arithmetic  24.9 us (11%)
  local copies, waits for them, and re-layouts  23.5 us (10%)
  matrix products  5.73 us (2%)
    all_gather x2, blocking collectives, fold_traces(): lax.all_gather(mine, 'wide', axis=2, tiled=True)  52 us
    ppermute x15, starting transfers between devices, with_halo(): before = lax.ppermute(last, axis, up)  47.9 us
    ppermute x15, waiting for transfers between devices, with_halo(): after = lax.ppermute(first, axis, down)  27 us
    ppermute x15, starting transfers between devices, with_halo(): after = lax.ppermute(first, axis, down)  19.4 us
    ppermute x15, waiting for transfers between devices, with_halo(): before = lax.ppermute(last, axis, up)  16.7 us
    mul x5, other arithmetic, apply_operator(): weighted = box_sum(padded * cond_pad) - conductance * center  11.6 us
    psum x2, blocking collectives, local(): summed = lax.psum(partial_rows, 'narrow')  10.5 us
    reshape x1, local copies, waits for them, and re-layouts, local(): plane = boundary_operator.reshape(tile_rows, BY, -1)  6.41 us
  transfers between devices with their start and end apart: 30, of which 11 were waited for; matrix products, arithmetic and copies ran while one was open for 6% of the time, Pallas kernels for 0%

commit v1 on v0

--- a/solution.py
+++ b/solution.py
@@ -12,6 +12,20 @@
 upper_edge = 1.75
 mass_ratio = 26.0
 couple_gain = 40.0
+
+
+def turn_rates(field, along_axis, ndim_at, own_rows):
+    ready = lax.psum(1, along_axis)
+    left_arr = lax.axis_index(along_axis)
+    newest, local_next = (ready, left_arr)
+    heap = [(it, (it - 1) % newest) for it in range(newest)]
+    then = field.shape[ndim_at]
+    low = field
+    current_arr = own_rows(low, local_next * then)
+    for d in range(1, newest):
+        low = lax.ppermute(low, along_axis, heap)
+        current_arr = current_arr + own_rows(low, (local_next + d) % newest * then)
+    return current_arr
 
 
 def with_halo(shard, sides, width):
@@ -68,11 +82,16 @@
 
 
 def fold_traces(mine, plane):
-    return jnp.einsum(
-        "ryx,kyx->rk",
-        plane,
-        lax.all_gather(mine, "wide", axis=2, tiled=True),
-        preferred_element_type=jnp.float32,
+    return turn_rates(
+        mine,
+        "wide",
+        2,
+        lambda shard_2, offset: jnp.einsum(
+            "ryx,kyx->rk",
+            lax.dynamic_slice_in_dim(plane, offset, shard_2.shape[2], axis=2),
+            shard_2,
+            preferred_element_type=jnp.float32,
+        ),
     )
 
 

time: 237 us -> 265 us (1.12)
  starting transfers between devices: 67.3 us -> 150 us
  blocking collectives: 69.3 us -> 17.2 us
  waiting for transfers between devices: 43.7 us -> 33.7 us
  local copies, waits for them, and re-layouts: 23.5 us -> 27.7 us
    ppermute x0 -> x14, starting transfers between devices: none -> 65.9 us  [turn_rates(): low = lax.ppermute(low, along_axis, heap)]
    all_gather x2 -> x0, blocking collectives: 52 us -> none  [fold_traces(): lax.all_gather(mine, 'wide', axis=2, tiled=True)]
    ppermute x15, waiting for transfers between devices: 27 us -> 7.71 us  [with_halo(): after = lax.ppermute(first, axis, down)]
    ppermute x15, starting transfers between devices: 47.9 us -> 64.1 us  [with_halo(): before = lax.ppermute(last, axis, up)]
    ppermute x0 -> x14, waiting for transfers between devices: none -> 10.8 us  [turn_rates(): low = lax.ppermute(low, along_axis, heap)]
    reshape x1 -> x0, local copies, waits for them, and re-layouts: 6.41 us -> none  [local(): plane = boundary_operator.reshape(tile_rows, BY, -1)]
    unnamed x38 -> x61, local copies, waits for them, and re-layouts: 6.24 us -> 12.6 us
    dynamic_slice x0 -> x1, local copies, waits for them, and re-layouts: none -> 4.37 us  [fold_traces(): lax.dynamic_slice_in_dim(plane, offset, shard_2.shape[2], axis=2)]
  transfers between devices with their start and end apart: 30 -> 44, of which waited for: 11 -> 21; matrix products, arithmetic and copies ran while one was open for 6% -> 10% of each run, Pallas kernels for 0% -> 0%
where the time goes in v1:
time: 265 us; the launch traced here: 264 us
  starting transfers between devices  150 us (57%)
  waiting for transfers between devices  33.7 us (13%)
  local copies, waits for them, and re-layouts  27.7 us (10%)
  other arithmetic  25.8 us (10%)
  blocking collectives  17.2 us (6%)
  matrix products  8.22 us (3%)
    ppermute x14, starting transfers between devices, turn_rates(): low = lax.ppermute(low, along_axis, heap)  65.9 us
    ppermute x15, starting transfers between devices, with_halo(): before = lax.ppermute(last, axis, up)  64.1 us
    ppermute x15, starting transfers between devices, with_halo(): after = lax.ppermute(first, axis, down)  19.5 us
    ppermute x15, waiting for transfers between devices, with_halo(): before = lax.ppermute(last, axis, up)  15.2 us
    unnamed x61, local copies, waits for them, and re-layouts  12.6 us
    mul x5, other arithmetic, apply_operator(): weighted = box_sum(padded * cond_pad) - conductance * center  11.5 us
    ppermute x14, waiting for transfers between devices, turn_rates(): low = lax.ppermute(low, along_axis, heap)  10.8 us
    psum x2, blocking collectives, local(): summed = lax.psum(partial_rows, 'narrow')  10.1 us
  transfers between devices with their start and end apart: 44, of which 21 were waited for; matrix products, arithmetic and copies ran while one was open for 10% of the time, Pallas kernels for 0%

profile of v1, /device:TPU:0, one launch (start us, length us, event | category | flops | bytes accessed | tf_op | source)
XLA Modules:
  0.0 263.7 jit_solution(11847850267165204872)
XLA Ops:
  2.2 6.7 %broadcast_multiply_fusion.5 = (f32[2,192,128]{2,1,0:T(8,128)}, f32[2,192,128]{2,1,0:T(8,128)S(1)}) fusion(f32[]{:T(128)} %bitcast.7, s32[2,192,128]{2,1,0:T(8,128)} %param.7, f32[]{:T(128)} %bitcast.6, f32[]{:T(128)} %bitcast.5, f32[]{:T(128)} %bitcast.4, f32[]{:T(128)} %bitcast.3, f32[]{:T(128)} %bitcast.2, f32[]{:T(128)} %bitcast.1, f32[]{:T(128)} %bitcast), kind=kLoop, calls=%fused_computation.157 | loop fusion | flops 1179648 | bytes 589856 | tf_op jit(solution)/shard_map/mul | solution.py:68
  15.8 5.5 %collective-permute-start.2 = (f32[4,192,1]{2,1,0:T(8,128)S(1)}, f32[4,192,1]{2,1,0:T(8,128)S(1)}, u32[]{:S(2)}, u32[]{:S(2)}) collective-permute-start(f32[4,192,1]{2,1,0:T(8,128)S(1)} %get-tuple-element.70), channel_id=1, source_target_pairs={{0,2},{2,4},{4,6},{6,8},{8,10},{10,12},{12,14},{1,3},{3,5},{5,7},{... | collective-permute-start | bytes 9224 | tf_op jit(solution)/shard_map/ppermute | solution.py:38
  21.3 7.7 %collective-permute-done.3 = f32[4,192,1]{2,1,0:T(8,128)S(1)} collective-permute-done((f32[4,192,1]{2,1,0:T(8,128)S(1)}, f32[4,192,1]{2,1,0:T(8,128)S(1)}, u32[]{:S(2)}, u32[]{:S(2)}) %collective-permute-start.3) | collective-permute-done | bytes 3104 | tf_op jit(solution)/shard_map/ppermute | solution.py:39
  29.0 8.6 %collective-permute-done.2 = f32[4,192,1]{2,1,0:T(8,128)S(1)} collective-permute-done((f32[4,192,1]{2,1,0:T(8,128)S(1)}, f32[4,192,1]{2,1,0:T(8,128)S(1)}, u32[]{:S(2)}, u32[]{:S(2)}) %collective-permute-start.2) | collective-permute-done | bytes 3104 | tf_op jit(solution)/shard_map/ppermute | solution.py:38
  53.3 5.0 %collective-permute-start.8 = (f32[2,4,192,1]{2,1,3,0:T(4,128)S(1)}, f32[2,4,192,1]{2,1,3,0:T(4,128)S(1)}, u32[]{:S(2)}, u32[]{:S(2)}) collective-permute-start(f32[2,4,192,1]{2,1,3,0:T(4,128)S(1)} %copy.19), channel_id=1, source_target_pairs={{0,2},{2,4},{4,6},{6,8},{8,10},{10,12},{12,14},{1,3},{3,5},{5,7},{... | collective-permute-start | bytes 18440 | tf_op jit(solution)/shard_map/ppermute | solution.py:38
  80.7 5.4 %collective-permute-start.14 = (f32[2,4,192,1]{2,1,3,0:T(4,128)S(1)}, f32[2,4,192,1]{2,1,3,0:T(4,128)S(1)}, u32[]{:S(2)}, u32[]{:S(2)}) collective-permute-start(f32[2,4,192,1]{2,1,3,0:T(4,128)S(1)} %copy.24), channel_id=1, source_target_pairs={{0,2},{2,4},{4,6},{6,8},{8,10},{10,12},{12,14},{1,3},{3,5},{5,7},{... | collective-permute-start | bytes 18440 | tf_op jit(solution)/shard_map/ppermute | solution.py:38
  86.3 7.0 %copy.64 = bf16[16,8,16,1024]{3,2,1,0:T(8,128)(2,1)} copy(bf16[16,8,16,1024]{3,1,2,0:T(8,128)(2,1)} %bitcast.121) | data formatting | bytes 8388608
  96.0 4.7 %collective-permute-start.16 = (f32[2,4,1,130]{3,2,0,1:T(1,128)S(1)}, f32[2,4,1,130]{3,2,0,1:T(1,128)S(1)}, u32[]{:S(2)}, u32[]{:S(2)}) collective-permute-start(f32[2,4,1,130]{3,2,0,1:T(1,128)S(1)} %get-tuple-element.48), channel_id=1, source_target_pairs={{0,1},{2,3},{4,5},{6,7},{8,9},{10,11},{12,13},{14,15},{16,17},{18,... | collective-permute-start | bytes 12488 | tf_op jit(solution)/shard_map/ppermute | solution.py:38
  112.0 4.6 %collective-permute-start.18 = (bf16[1,16,128]{2,1,0:T(8,128)(2,1)S(1)}, bf16[1,16,128]{2,1,0:T(8,128)(2,1)S(1)}, u32[]{:S(2)}, u32[]{:S(2)}) collective-permute-start(bf16[1,16,128]{2,1,0:T(8,128)(2,1)S(1)} %constant_dynamic-slice_fusion.10), channel_id=1, source_target_pairs={{0,14},{2,0},{4,2},{6,4},{8,6},{10,8},{12,10},{14,12},{1,15},{3,1}... | collective-permute-start | bytes 12296 | tf_op jit(solution)/shard_map/ppermute | solution.py:26
  126.5 5.0 %collective-permute-start.20 = (bf16[1,16,128]{2,1,0:T(8,128)(2,1)S(1)}, bf16[1,16,128]{2,1,0:T(8,128)(2,1)S(1)}, u32[]{:S(2)}, u32[]{:S(2)}) collective-permute-start(bf16[1,16,128]{2,1,0:T(8,128)(2,1)S(1)} %collective-permute-done.19), channel_id=1, source_target_pairs={{0,14},{2,0},{4,2},{6,4},{8,6},{10,8},{12,10},{14,12},{1,15},{3,1}... | collective-permute-start | bytes 12296 | tf_op jit(solution)/shard_map/ppermute | solution.py:26
  132.8 5.0 %collective-permute-start.21 = (bf16[1,16,128]{2,1,0:T(8,128)(2,1)S(1)}, bf16[1,16,128]{2,1,0:T(8,128)(2,1)S(1)}, u32[]{:S(2)}, u32[]{:S(2)}) collective-permute-start(bf16[1,16,128]{2,1,0:T(8,128)(2,1)S(1)} %collective-permute-done.20), channel_id=1, source_target_pairs={{0,14},{2,0},{4,2},{6,4},{8,6},{10,8},{12,10},{14,12},{1,15},{3,1}... | collective-permute-start | bytes 12296 | tf_op jit(solution)/shard_map/ppermute | solution.py:26
  139.1 5.0 %collective-permute-start.22 = (bf16[1,16,128]{2,1,0:T(8,128)(2,1)S(1)}, bf16[1,16,128]{2,1,0:T(8,128)(2,1)S(1)}, u32[]{:S(2)}, u32[]{:S(2)}) collective-permute-start(bf16[1,16,128]{2,1,0:T(8,128)(2,1)S(1)} %collective-permute-done.21), channel_id=1, source_target_pairs={{0,14},{2,0},{4,2},{6,4},{8,6},{10,8},{12,10},{14,12},{1,15},{3,1}... | collective-permute-start | bytes 12296 | tf_op jit(solution)/shard_map/ppermute | solution.py:26
  145.4 5.0 %collective-permute-start.23 = (bf16[1,16,128]{2,1,0:T(8,128)(2,1)S(1)}, bf16[1,16,128]{2,1,0:T(8,128)(2,1)S(1)}, u32[]{:S(2)}, u32[]{:S(2)}) collective-permute-start(bf16[1,16,128]{2,1,0:T(8,128)(2,1)S(1)} %collective-permute-done.22), channel_id=1, source_target_pairs={{0,14},{2,0},{4,2},{6,4},{8,6},{10,8},{12,10},{14,12},{1,15},{3,1}... | collective-permute-start | bytes 12296 | tf_op jit(solution)/shard_map/ppermute | solution.py:26
  151.7 5.0 %collective-permute-start.24 = (bf16[1,16,128]{2,1,0:T(8,128)(2,1)S(1)}, bf16[1,16,128]{2,1,0:T(8,128)(2,1)S(1)}, u32[]{:S(2)}, u32[]{:S(2)}) collective-permute-start(bf16[1,16,128]{2,1,0:T(8,128)(2,1)S(1)} %collective-permute-done.23), channel_id=1, source_target_pairs={{0,14},{2,0},{4,2},{6,4},{8,6},{10,8},{12,10},{14,12},{1,15},{3,1}... | collective-permute-start | bytes 12296 | tf_op jit(solution)/shard_map/ppermute | solution.py:26
  158.2 4.9 %psum.29 = f32[128,1]{0,1:T(1,128)S(1)} all-reduce(f32[128,1]{0,1:T(1,128)S(1)} %fusion.9), channel_id=1, replica_groups=mesh['vol'=2,'wide'=8,'narrow'=2] {'narrow'}, use_global_device_ids=true, to_apply=%region_1.2 | all-reduce | flops 128 | bytes 1024 | tf_op jit(solution)/shard_map/psum | solution.py:126
  165.9 4.5 %collective-permute-start.27 = (f32[2,4,192,1]{2,1,3,0:T(4,128)S(1)}, f32[2,4,192,1]{2,1,3,0:T(4,128)S(1)}, u32[]{:S(2)}, u32[]{:S(2)}) collective-permute-start(f32[2,4,192,1]{2,1,3,0:T(4,128)S(1)} %copy.31), channel_id=1, source_target_pairs={{0,2},{2,4},{4,6},{6,8},{8,10},{10,12},{12,14},{1,3},{3,5},{5,7},{... | collective-permute-start | bytes 18440 | tf_op jit(solution)/shard_map/ppermute | solution.py:38
  201.9 4.8 %collective-permute-start.35 = (f32[2,4,1,130]{3,2,0,1:T(1,128)S(1)}, f32[2,4,1,130]{3,2,0,1:T(1,128)S(1)}, u32[]{:S(2)}, u32[]{:S(2)}) collective-permute-start(f32[2,4,1,130]{3,2,0,1:T(1,128)S(1)} %get-tuple-element.44), channel_id=1, source_target_pairs={{0,1},{2,3},{4,5},{6,7},{8,9},{10,11},{12,13},{14,15},{16,17},{18,... | collective-permute-start | bytes 12488 | tf_op jit(solution)/shard_map/ppermute | solution.py:38
  213.9 4.7 %collective-permute-start.37 = (bf16[1,16,128]{2,1,0:T(8,128)(2,1)S(1)}, bf16[1,16,128]{2,1,0:T(8,128)(2,1)S(1)}, u32[]{:S(2)}, u32[]{:S(2)}) collective-permute-start(bf16[1,16,128]{2,1,0:T(8,128)(2,1)S(1)} %constant_dynamic-slice_fusion.1), channel_id=1, source_target_pairs={{0,14},{2,0},{4,2},{6,4},{8,6},{10,8},{12,10},{14,12},{1,15},{3,1}... | collective-permute-start | bytes 12296 | tf_op jit(solution)/shard_map/ppermute | solution.py:26
  226.2 5.0 %collective-permute-start.39 = (bf16[1,16,128]{2,1,0:T(8,128)(2,1)S(1)}, bf16[1,16,128]{2,1,0:T(8,128)(2,1)S(1)}, u32[]{:S(2)}, u32[]{:S(2)}) collective-permute-start(bf16[1,16,128]{2,1,0:T(8,128)(2,1)S(1)} %collective-permute-done.38), channel_id=1, source_target_pairs={{0,14},{2,0},{4,2},{6,4},{8,6},{10,8},{12,10},{14,12},{1,15},{3,1}... | collective-permute-start | bytes 12296 | tf_op jit(solution)/shard_map/ppermute | solution.py:26
  232.5 5.0 %collective-permute-start.40 = (bf16[1,16,128]{2,1,0:T(8,128)(2,1)S(1)}, bf16[1,16,128]{2,1,0:T(8,128)(2,1)S(1)}, u32[]{:S(2)}, u32[]{:S(2)}) collective-permute-start(bf16[1,16,128]{2,1,0:T(8,128)(2,1)S(1)} %collective-permute-done.39), channel_id=1, source_target_pairs={{0,14},{2,0},{4,2},{6,4},{8,6},{10,8},{12,10},{14,12},{1,15},{3,1}... | collective-permute-start | bytes 12296 | tf_op jit(solution)/shard_map/ppermute | solution.py:26
  238.8 5.0 %collective-permute-start.41 = (bf16[1,16,128]{2,1,0:T(8,128)(2,1)S(1)}, bf16[1,16,128]{2,1,0:T(8,128)(2,1)S(1)}, u32[]{:S(2)}, u32[]{:S(2)}) collective-permute-start(bf16[1,16,128]{2,1,0:T(8,128)(2,1)S(1)} %collective-permute-done.40), channel_id=1, source_target_pairs={{0,14},{2,0},{4,2},{6,4},{8,6},{10,8},{12,10},{14,12},{1,15},{3,1}... | collective-permute-start | bytes 12296 | tf_op jit(solution)/shard_map/ppermute | solution.py:26
  245.1 5.0 %collective-permute-start.42 = (bf16[1,16,128]{2,1,0:T(8,128)(2,1)S(1)}, bf16[1,16,128]{2,1,0:T(8,128)(2,1)S(1)}, u32[]{:S(2)}, u32[]{:S(2)}) collective-permute-start(bf16[1,16,128]{2,1,0:T(8,128)(2,1)S(1)} %collective-permute-done.41), channel_id=1, source_target_pairs={{0,14},{2,0},{4,2},{6,4},{8,6},{10,8},{12,10},{14,12},{1,15},{3,1}... | collective-permute-start | bytes 12296 | tf_op jit(solution)/shard_map/ppermute | solution.py:26
  251.4 5.0 %collective-permute-start.43 = (bf16[1,16,128]{2,1,0:T(8,128)(2,1)S(1)}, bf16[1,16,128]{2,1,0:T(8,128)(2,1)S(1)}, u32[]{:S(2)}, u32[]{:S(2)}) collective-permute-start(bf16[1,16,128]{2,1,0:T(8,128)(2,1)S(1)} %collective-permute-done.42), channel_id=1, source_target_pairs={{0,14},{2,0},{4,2},{6,4},{8,6},{10,8},{12,10},{14,12},{1,15},{3,1}... | collective-permute-start | bytes 12296 | tf_op jit(solution)/shard_map/ppermute | solution.py:26
  257.9 5.2 %psum.31 = f32[128,1]{0,1:T(1,128)S(1)} all-reduce(f32[128,1]{0,1:T(1,128)S(1)} %fusion.1), channel_id=1, replica_groups=mesh['vol'=2,'wide'=8,'narrow'=2] {'narrow'}, use_global_device_ids=true, to_apply=%region_3.4 | all-reduce | flops 128 | bytes 1024 | tf_op jit(solution)/shard_map/psum | solution.py:126
  (223 shorter events, 133.0 us)
Async XLA Ops:
  14.5 14.5 %collective-permute-start.3 = (f32[4,192,1]{2,1,0:T(8,128)S(1)}, f32[4,192,1]{2,1,0:T(8,128)S(1)}, u32[]{:S(2)}, u32[]{:S(2)}) collective-permute-start(f32[4,192,1]{2,1,0:T(8,128)S(1)} %get-tuple-element.71), channel_id=1, source_target_pairs={{2,0},{4,2},{6,4},{8,6},{10,8},{12,10},{14,12},{3,1},{5,3},{7,5},{... | collective-permute-start | bytes 9224 | tf_op jit(solution)/shard_map/ppermute | solution.py:39
  15.8 21.8 %collective-permute-start.2 = (f32[4,192,1]{2,1,0:T(8,128)S(1)}, f32[4,192,1]{2,1,0:T(8,128)S(1)}, u32[]{:S(2)}, u32[]{:S(2)}) collective-permute-start(f32[4,192,1]{2,1,0:T(8,128)S(1)} %get-tuple-element.70), channel_id=1, source_target_pairs={{0,2},{2,4},{4,6},{6,8},{8,10},{10,12},{12,14},{1,3},{3,5},{5,7},{... | collective-permute-start | bytes 9224 | tf_op jit(solution)/shard_map/ppermute | solution.py:38
  37.7 10.2 %collective-permute-start.5 = (f32[4,1,130]{2,1,0:T(1,128)S(1)}, f32[4,1,130]{2,1,0:T(1,128)S(1)}, u32[]{:S(2)}, u32[]{:S(2)}) collective-permute-start(f32[4,1,130]{2,1,0:T(1,128)S(1)} %get-tuple-element.53), channel_id=1, source_target_pairs={{1,0},{3,2},{5,4},{7,6},{9,8},{11,10},{13,12},{15,14},{17,16},{19,... | collective-permute-start | bytes 6248 | tf_op jit(solution)/shard_map/ppermute | solution.py:39
  39.0 8.9 %collective-permute-start.4 = (f32[4,1,130]{2,1,0:T(1,128)S(1)}, f32[4,1,130]{2,1,0:T(1,128)S(1)}, u32[]{:S(2)}, u32[]{:S(2)}) collective-permute-start(f32[4,1,130]{2,1,0:T(1,128)S(1)} %get-tuple-element.52), channel_id=1, source_target_pairs={{0,1},{2,3},{4,5},{6,7},{8,9},{10,11},{12,13},{14,15},{16,17},{18,... | collective-permute-start | bytes 6248 | tf_op jit(solution)/shard_map/ppermute | solution.py:38
  51.6 7.5 %collective-permute-start.9 = (f32[2,4,192,1]{2,1,3,0:T(4,128)S(1)}, f32[2,4,192,1]{2,1,3,0:T(4,128)S(1)}, u32[]{:S(2)}, u32[]{:S(2)}) collective-permute-start(f32[2,4,192,1]{2,1,3,0:T(4,128)S(1)} %copy.20), channel_id=1, source_target_pairs={{2,0},{4,2},{6,4},{8,6},{10,8},{12,10},{14,12},{3,1},{5,3},{7,5},{... | collective-permute-start | bytes 18440 | tf_op jit(solution)/shard_map/ppermute | solution.py:39
  53.3 6.3 %collective-permute-start.8 = (f32[2,4,192,1]{2,1,3,0:T(4,128)S(1)}, f32[2,4,192,1]{2,1,3,0:T(4,128)S(1)}, u32[]{:S(2)}, u32[]{:S(2)}) collective-permute-start(f32[2,4,192,1]{2,1,3,0:T(4,128)S(1)} %copy.19), channel_id=1, source_target_pairs={{0,2},{2,4},{4,6},{6,8},{8,10},{10,12},{12,14},{1,3},{3,5},{5,7},{... | collective-permute-start | bytes 18440 | tf_op jit(solution)/shard_map/ppermute | solution.py:38
  60.1 7.0 %collective-permute-start.11 = (f32[2,4,1,130]{3,2,0,1:T(1,128)S(1)}, f32[2,4,1,130]{3,2,0,1:T(1,128)S(1)}, u32[]{:S(2)}, u32[]{:S(2)}) collective-permute-start(f32[2,4,1,130]{3,2,0,1:T(1,128)S(1)} %get-tuple-element.51), channel_id=1, source_target_pairs={{1,0},{3,2},{5,4},{7,6},{9,8},{11,10},{13,12},{15,14},{17,16},{19,... | collective-permute-start | bytes 12488 | tf_op jit(solution)/shard_map/ppermute | solution.py:39
  79.1 14.2 %collective-permute-start.15 = (f32[2,4,192,1]{2,1,3,0:T(4,128)S(1)}, f32[2,4,192,1]{2,1,3,0:T(4,128)S(1)}, u32[]{:S(2)}, u32[]{:S(2)}) collective-permute-start(f32[2,4,192,1]{2,1,3,0:T(4,128)S(1)} %copy.25), channel_id=1, source_target_pairs={{2,0},{4,2},{6,4},{8,6},{10,8},{12,10},{14,12},{3,1},{5,3},{7,5},{... | collective-permute-start | bytes 18440 | tf_op jit(solution)/shard_map/ppermute | solution.py:39
  80.7 12.8 %collective-permute-start.14 = (f32[2,4,192,1]{2,1,3,0:T(4,128)S(1)}, f32[2,4,192,1]{2,1,3,0:T(4,128)S(1)}, u32[]{:S(2)}, u32[]{:S(2)}) collective-permute-start(f32[2,4,192,1]{2,1,3,0:T(4,128)S(1)} %copy.24), channel_id=1, source_target_pairs={{0,2},{2,4},{4,6},{6,8},{8,10},{10,12},{12,14},{1,3},{3,5},{5,7},{... | collective-permute-start | bytes 18440 | tf_op jit(solution)/shard_map/ppermute | solution.py:38
  94.7 10.4 %collective-permute-start.17 = (f32[2,4,1,130]{3,2,0,1:T(1,128)S(1)}, f32[2,4,1,130]{3,2,0,1:T(1,128)S(1)}, u32[]{:S(2)}, u32[]{:S(2)}) collective-permute-start(f32[2,4,1,130]{3,2,0,1:T(1,128)S(1)} %get-tuple-element.49), channel_id=1, source_target_pairs={{1,0},{3,2},{5,4},{7,6},{9,8},{11,10},{13,12},{15,14},{17,16},{19,... | collective-permute-start | bytes 12488 | tf_op jit(solution)/shard_map/ppermute | solution.py:39
  96.0 9.1 %collective-permute-start.16 = (f32[2,4,1,130]{3,2,0,1:T(1,128)S(1)}, f32[2,4,1,130]{3,2,0,1:T(1,128)S(1)}, u32[]{:S(2)}, u32[]{:S(2)}) collective-permute-start(f32[2,4,1,130]{3,2,0,1:T(1,128)S(1)} %get-tuple-element.48), channel_id=1, source_target_pairs={{0,1},{2,3},{4,5},{6,7},{8,9},{10,11},{12,13},{14,15},{16,17},{18,... | collective-permute-start | bytes 12488 | tf_op jit(solution)/shard_map/ppermute | solution.py:38
  112.0 10.5 %collective-permute-start.18 = (bf16[1,16,128]{2,1,0:T(8,128)(2,1)S(1)}, bf16[1,16,128]{2,1,0:T(8,128)(2,1)S(1)}, u32[]{:S(2)}, u32[]{:S(2)}) collective-permute-start(bf16[1,16,128]{2,1,0:T(8,128)(2,1)S(1)} %constant_dynamic-slice_fusion.10), channel_id=1, source_target_pairs={{0,14},{2,0},{4,2},{6,4},{8,6},{10,8},{12,10},{14,12},{1,15},{3,1}... | collective-permute-start | bytes 12296 | tf_op jit(solution)/shard_map/ppermute | solution.py:26
  116.6 46.5 %collective-permute-start.26 = (f32[2,1,192,128]{3,2,0,1:T(8,128)S(1)}, f32[2,1,192,128]{3,2,0,1:T(8,128)S(1)}, u32[]{:S(2)}, u32[]{:S(2)}) collective-permute-start(f32[2,1,192,128]{3,2,0,1:T(8,128)S(1)} %get-tuple-element.65), channel_id=1, source_target_pairs={{16,0},{17,1},{18,2},{19,3},{20,4},{21,5},{22,6},{23,7},{24,8},{25... | collective-permute-start | bytes 589832 | tf_op jit(solution)/shard_map/ppermute | solution.py:39
  118.1 45.1 %collective-permute-start.25 = (f32[2,1,192,128]{3,2,0,1:T(8,128)S(1)}, f32[2,1,192,128]{3,2,0,1:T(8,128)S(1)}, u32[]{:S(2)}, u32[]{:S(2)}) collective-permute-start(f32[2,1,192,128]{3,2,0,1:T(8,128)S(1)} %get-tuple-element.64), channel_id=1, source_target_pairs={{0,16},{1,17},{2,18},{3,19},{4,20},{5,21},{6,22},{7,23},{8,24},{9,... | collective-permute-start | bytes 589832 | tf_op jit(solution)/shard_map/ppermute | solution.py:38
  132.8 6.3 %collective-permute-start.21 = (bf16[1,16,128]{2,1,0:T(8,128)(2,1)S(1)}, bf16[1,16,128]{2,1,0:T(8,128)(2,1)S(1)}, u32[]{:S(2)}, u32[]{:S(2)}) collective-permute-start(bf16[1,16,128]{2,1,0:T(8,128)(2,1)S(1)} %collective-permute-done.20), channel_id=1, source_target_pairs={{0,14},{2,0},{4,2},{6,4},{8,6},{10,8},{12,10},{14,12},{1,15},{3,1}... | collective-permute-start | bytes 12296 | tf_op jit(solution)/shard_map/ppermute | solution.py:26
  139.1 6.3 %collective-permute-start.22 = (bf16[1,16,128]{2,1,0:T(8,128)(2,1)S(1)}, bf16[1,16,128]{2,1,0:T(8,128)(2,1)S(1)}, u32[]{:S(2)}, u32[]{:S(2)}) collective-permute-start(bf16[1,16,128]{2,1,0:T(8,128)(2,1)S(1)} %collective-permute-done.21), channel_id=1, source_target_pairs={{0,14},{2,0},{4,2},{6,4},{8,6},{10,8},{12,10},{14,12},{1,15},{3,1}... | collective-permute-start | bytes 12296 | tf_op jit(solution)/shard_map/ppermute | solution.py:26
  145.4 6.3 %collective-permute-start.23 = (bf16[1,16,128]{2,1,0:T(8,128)(2,1)S(1)}, bf16[1,16,128]{2,1,0:T(8,128)(2,1)S(1)}, u32[]{:S(2)}, u32[]{:S(2)}) collective-permute-start(bf16[1,16,128]{2,1,0:T(8,128)(2,1)S(1)} %collective-permute-done.22), channel_id=1, source_target_pairs={{0,14},{2,0},{4,2},{6,4},{8,6},{10,8},{12,10},{14,12},{1,15},{3,1}... | collective-permute-start | bytes 12296 | tf_op jit(solution)/shard_map/ppermute | solution.py:26
  151.7 6.3 %collective-permute-start.24 = (bf16[1,16,128]{2,1,0:T(8,128)(2,1)S(1)}, bf16[1,16,128]{2,1,0:T(8,128)(2,1)S(1)}, u32[]{:S(2)}, u32[]{:S(2)}) collective-permute-start(bf16[1,16,128]{2,1,0:T(8,128)(2,1)S(1)} %collective-permute-done.23), channel_id=1, source_target_pairs={{0,14},{2,0},{4,2},{6,4},{8,6},{10,8},{12,10},{14,12},{1,15},{3,1}... | collective-permute-start | bytes 12296 | tf_op jit(solution)/shard_map/ppermute | solution.py:26
  164.3 8.1 %collective-permute-start.28 = (f32[2,4,192,1]{2,1,3,0:T(4,128)S(1)}, f32[2,4,192,1]{2,1,3,0:T(4,128)S(1)}, u32[]{:S(2)}, u32[]{:S(2)}) collective-permute-start(f32[2,4,192,1]{2,1,3,0:T(4,128)S(1)} %copy.32), channel_id=1, source_target_pairs={{2,0},{4,2},{6,4},{8,6},{10,8},{12,10},{14,12},{3,1},{5,3},{7,5},{... | collective-permute-start | bytes 18440 | tf_op jit(solution)/shard_map/ppermute | solution.py:39
  165.9 6.8 %collective-permute-start.27 = (f32[2,4,192,1]{2,1,3,0:T(4,128)S(1)}, f32[2,4,192,1]{2,1,3,0:T(4,128)S(1)}, u32[]{:S(2)}, u32[]{:S(2)}) collective-permute-start(f32[2,4,192,1]{2,1,3,0:T(4,128)S(1)} %copy.31), channel_id=1, source_target_pairs={{0,2},{2,4},{4,6},{6,8},{8,10},{10,12},{12,14},{1,3},{3,5},{5,7},{... | collective-permute-start | bytes 18440 | tf_op jit(solution)/shard_map/ppermute | solution.py:38
  213.9 6.7 %collective-permute-start.37 = (bf16[1,16,128]{2,1,0:T(8,128)(2,1)S(1)}, bf16[1,16,128]{2,1,0:T(8,128)(2,1)S(1)}, u32[]{:S(2)}, u32[]{:S(2)}) collective-permute-start(bf16[1,16,128]{2,1,0:T(8,128)(2,1)S(1)} %constant_dynamic-slice_fusion.1), channel_id=1, source_target_pairs={{0,14},{2,0},{4,2},{6,4},{8,6},{10,8},{12,10},{14,12},{1,15},{3,1}... | collective-permute-start | bytes 12296 | tf_op jit(solution)/shard_map/ppermute | solution.py:26
  232.5 6.3 %collective-permute-start.40 = (bf16[1,16,128]{2,1,0:T(8,128)(2,1)S(1)}, bf16[1,16,128]{2,1,0:T(8,128)(2,1)S(1)}, u32[]{:S(2)}, u32[]{:S(2)}) collective-permute-start(bf16[1,16,128]{2,1,0:T(8,128)(2,1)S(1)} %collective-permute-done.39), channel_id=1, source_target_pairs={{0,14},{2,0},{4,2},{6,4},{8,6},{10,8},{12,10},{14,12},{1,15},{3,1}... | collective-permute-start | bytes 12296 | tf_op jit(solution)/shard_map/ppermute | solution.py:26
  238.8 6.3 %collective-permute-start.41 = (bf16[1,16,128]{2,1,0:T(8,128)(2,1)S(1)}, bf16[1,16,128]{2,1,0:T(8,128)(2,1)S(1)}, u32[]{:S(2)}, u32[]{:S(2)}) collective-permute-start(bf16[1,16,128]{2,1,0:T(8,128)(2,1)S(1)} %collective-permute-done.40), channel_id=1, source_target_pairs={{0,14},{2,0},{4,2},{6,4},{8,6},{10,8},{12,10},{14,12},{1,15},{3,1}... | collective-permute-start | bytes 12296 | tf_op jit(solution)/shard_map/ppermute | solution.py:26
  245.1 6.3 %collective-permute-start.42 = (bf16[1,16,128]{2,1,0:T(8,128)(2,1)S(1)}, bf16[1,16,128]{2,1,0:T(8,128)(2,1)S(1)}, u32[]{:S(2)}, u32[]{:S(2)}) collective-permute-start(bf16[1,16,128]{2,1,0:T(8,128)(2,1)S(1)} %collective-permute-done.41), channel_id=1, source_target_pairs={{0,14},{2,0},{4,2},{6,4},{8,6},{10,8},{12,10},{14,12},{1,15},{3,1}... | collective-permute-start | bytes 12296 | tf_op jit(solution)/shard_map/ppermute | solution.py:26
  (49 other events, 530.3 us)
